TPU v7x, 512 devices: a whole 4x8x8 slice. The times are simulated.
512 devices in a mesh: blk: 64 (over z, y_lo, core), rep: 8 (over y_hi, x).
Axes of the slice: x: 4, y: 8 (y_hi: 2, y_lo: 4; y = y_hi * 4 + y_lo), z: 8, core: 2. Of those that a mesh axis runs over, the one named last changes fastest.
Arguments:
- points: float32 [16, 81920], P(None, ('blk', 'rep')), may hold values from -3 to 3
- vectors: float32 [32, 81920], P(None, ('blk', 'rep')), may hold values from -1.2 to 1.2
- lengthscales: float32 [16], replicated, may hold values from 0.6 to 1.6
Outputs:
- product: float32 [32, 81920], P(None, ('blk', 'rep'))
All inputs are finite; a program needn't handle non-finite values.
Results may differ from a plain program's by a relative error of at most 0.0003.
Values sent between devices are 32-bit elements; how exact they have to be, the bound alone decides.
A program may use at most 64 MiB of HBM per device.

v0:
```python
import jax
import jax.numpy as jnp
from jax import lax
from jax.sharding import PartitionSpec as P


def shifted(value, axis, steps):
    count = lax.axis_size(axis)
    pairs = [(source, (source + steps) % count) for source in range(count)]
    return lax.ppermute(value, axis, pairs)


def matern_tile(col_z, row_z, row_sq):
    col_sq = jnp.sum(col_z * col_z, axis=0)
    cross = lax.dot_general(
        col_z,
        row_z,
        (((0,), (0,)), ((), ())),
        precision=lax.Precision.HIGHEST,
        preferred_element_type=jnp.float32,
    )
    sqdist = jnp.maximum(col_sq[:, None] + row_sq[None, :] - 2.0 * cross, 0.0)
    svalue = jnp.sqrt(5.0 * sqdist)
    return (1.0 + svalue + svalue * svalue / 3.0) * jnp.exp(-svalue)


def rows_times(col_v, kernel):
    return lax.dot(
        col_v, kernel, precision=lax.Precision.HIGHEST, preferred_element_type=jnp.float32
    )


def cols_times(row_v, kernel):
    return lax.dot_general(
        row_v,
        kernel,
        (((1,), (1,)), ((), ())),
        precision=lax.Precision.HIGHEST,
        preferred_element_type=jnp.float32,
    )


def per_device(points, vectors, lengthscales):
    local_z = points / lengthscales[:, None]
    row_z, row_v = (
        lax.all_gather(local_z, "rep", axis=1, tiled=True),
        lax.all_gather(vectors, "rep", axis=1, tiled=True),
    )
    row_sq = jnp.sum(row_z * row_z, axis=0)
    half = lax.axis_size("blk") // 2
    row_acc = rows_times(vectors, matern_tile(local_z, row_z, row_sq))

    def cycle_step(step, carry):
        col_z, col_v, travel, row_total = carry
        col_z, col_v, travel = shifted((col_z, col_v, travel), "blk", 1)
        kernel = matern_tile(col_z, row_z, row_sq)
        return (
            col_z,
            col_v,
            travel + cols_times(row_v, kernel),
            row_total + rows_times(col_v, kernel),
        )

    start = (local_z, vectors, jnp.zeros_like(vectors), row_acc)
    col_z, col_v, travel, row_acc = lax.fori_loop(1, half, cycle_step, start)
    col_z, col_v = shifted((col_z, col_v), "blk", 1)
    returned = shifted(travel, "blk", 1 - half)
    row_acc = row_acc + rows_times(col_v, matern_tile(col_z, row_z, row_sq))
    return lax.psum_scatter(row_acc, "rep", scatter_dimension=1, tiled=True) + returned


def solution(mesh):
    return jax.shard_map(
        per_device,
        mesh=mesh,
        in_specs=(P(None, ("blk", "rep")), P(None, ("blk", "rep")), P()),
        out_specs=P(None, ("blk", "rep")),
        check_vma=False,
    )
```

profile of v0, /device:TPU:2, one launch (start us, length us, event | category | flops | bytes accessed | tf_op | source)
XLA Modules:
  0.0 664.6 jit_solution(17798006925289154229)
XLA Ops:
  8.1 44.3 %all-gather = f32[8,160,16]{1,2,0:T(8,128)S(1)} all-gather(f32[1,160,16]{1,2,0:T(8,128)S(1)} %bitcast.59), channel_id=1, replica_groups=mesh['blk'=64,'rep'=8] {'rep'}, dimensions={0}, use_global_device_ids=true | all-gather | bytes 92160 | tf_op jit(solution)/shard_map/all_gather | solution.py:46
  54.4 44.0 %all-gather.1 = f32[8,160,32]{1,2,0:T(8,128)S(1)} all-gather(f32[1,160,32]{1,2,0:T(8,128)S(1)} %bitcast.57), channel_id=1, replica_groups=mesh['blk'=64,'rep'=8] {'rep'}, dimensions={0}, use_global_device_ids=true | all-gather | bytes 184320 | tf_op jit(solution)/shard_map/all_gather | solution.py:47
  98.7 449.9 %while.17 = (s32[]{:T(128)}, f32[16,160]{1,0:T(8,128)S(1)}, f32[32,160]{1,0:T(8,128)S(1)}, f32[32,160]{1,0:T(8,128)S(1)}, f32[32,1280]{1,0:T(8,128)S(1)}, /*inde...) while((s32[]{:T(128)}, f32[16,160]{1,0:T(8,128)S(1)}, ...), condition=%wide.region_4.0_spmd.clone, body=%wide.region_2.0_spmd.clone.sunk | while | flops 198916960 | bytes 3426791 | solution.py:65
  109.0 3.6 collective-permute-done.1
  119.8 3.2 collective-permute-done
  124.3 2.8 collective-permute-done.1
  134.3 3.2 collective-permute-done
  138.8 2.8 collective-permute-done.1
  148.8 3.2 collective-permute-done
  153.3 2.8 collective-permute-done.1
  163.3 3.2 collective-permute-done
  177.8 3.2 collective-permute-done
  182.2 2.8 collective-permute-done.1
  192.3 3.2 collective-permute-done
  196.7 2.8 collective-permute-done.1
  206.8 3.2 collective-permute-done
  211.2 2.8 collective-permute-done.1
  221.2 3.2 collective-permute-done
  225.7 2.8 collective-permute-done.1
  235.7 3.2 collective-permute-done
  240.2 2.8 collective-permute-done.1
  250.2 3.2 collective-permute-done
  254.7 2.8 collective-permute-done.1
  264.7 3.2 collective-permute-done
  269.2 2.8 collective-permute-done.1
  279.2 3.2 collective-permute-done
  293.7 3.2 collective-permute-done
  298.1 2.8 collective-permute-done.1
  308.2 3.2 collective-permute-done
  312.6 2.8 collective-permute-done.1
  322.7 3.2 collective-permute-done
  327.1 2.8 collective-permute-done.1
  337.1 3.2 collective-permute-done
  341.6 2.8 collective-permute-done.1
  351.6 3.2 collective-permute-done
  356.1 2.8 collective-permute-done.1
  366.1 3.2 collective-permute-done
  370.6 2.8 collective-permute-done.1
  380.6 3.2 collective-permute-done
  385.1 2.8 collective-permute-done.1
  395.1 3.2 collective-permute-done
  399.5 2.8 collective-permute-done.1
  409.6 3.2 collective-permute-done
  414.0 2.8 collective-permute-done.1
  424.1 3.2 collective-permute-done
  428.5 2.8 collective-permute-done.1
  438.6 3.2 collective-permute-done
  443.0 2.8 collective-permute-done.1
  453.0 3.2 collective-permute-done
  457.5 2.8 collective-permute-done.1
  467.5 3.2 collective-permute-done
  472.0 2.8 collective-permute-done.1
  482.0 3.2 collective-permute-done
  486.5 2.8 collective-permute-done.1
  496.5 3.2 collective-permute-done
  501.0 2.8 collective-permute-done.1
  511.0 3.2 collective-permute-done
  515.4 2.8 collective-permute-done.1
  525.5 3.2 collective-permute-done
  540.0 3.2 collective-permute-done
  544.4 2.8 collective-permute-done.1
  552.5 5.1 collective-permute-done.4
  562.3 4.2 collective-permute-start.5
  566.5 89.7 %reduce-scatter.4.cloned.1.call-done = f32[160,32]{1,0:T(8,128)} async-done(((f32[1280,32]{1,0:T(8,128)}), f32[160,32]{1,0:T(8,128)}) %reduce-scatter.4.cloned.1.call-update) | async-done | bytes 20496
  (371 shorter events, 287.9 us)
Async XLA Ops:
  6.5 649.6 %reduce-scatter.4.cloned.1.call-start = ((), (), s32[]{:S(2)}) async-start(), calls=%async_computation.1 | async-start | bytes 737280
  100.7 12.5 %collective-permute-start.2 = (f32[32,160]{1,0:T(8,128)S(1)}, f32[32,160]{1,0:T(8,128)S(1)}, u32[]{:S(2)}, u32[]{:S(2)}) collective-permute-start(f32[32,160]{1,0:T(8,128)S(1)} %broadcast_select_fusion.2), channel_id=1, source_target_pairs={{0,8},{8,16},{16,24},{24,32},{32,40},{40,48},{48,56},{56,64},{64,7... | collective-permute-start | bytes 61448 | tf_op jit(solution)/shard_map/while/body/eval_jaxpr/ppermute | solution.py:10
  103.4 9.1 %collective-permute-start.1 = (f32[32,160]{1,0:T(8,128)S(1)}, f32[32,160]{1,0:T(8,128)S(1)}, u32[]{:S(2)}, u32[]{:S(2)}) collective-permute-start(f32[32,160]{1,0:T(8,128)S(1)} %get-tuple-element.160), channel_id=1, source_target_pairs={{0,8},{8,16},{16,24},{24,32},{32,40},{40,48},{48,56},{56,64},{64,7... | collective-permute-start | bytes 61448 | tf_op jit(solution)/shard_map/while/body/eval_jaxpr/ppermute | solution.py:10
  116.0 11.7 %collective-permute-start.2 = (f32[32,160]{1,0:T(8,128)S(1)}, f32[32,160]{1,0:T(8,128)S(1)}, u32[]{:S(2)}, u32[]{:S(2)}) collective-permute-start(f32[32,160]{1,0:T(8,128)S(1)} %broadcast_select_fusion.2), channel_id=1, source_target_pairs={{0,8},{8,16},{16,24},{24,32},{32,40},{40,48},{48,56},{56,64},{64,7... | collective-permute-start | bytes 61448 | tf_op jit(solution)/shard_map/while/body/eval_jaxpr/ppermute | solution.py:10
  117.9 9.1 %collective-permute-start.1 = (f32[32,160]{1,0:T(8,128)S(1)}, f32[32,160]{1,0:T(8,128)S(1)}, u32[]{:S(2)}, u32[]{:S(2)}) collective-permute-start(f32[32,160]{1,0:T(8,128)S(1)} %get-tuple-element.160), channel_id=1, source_target_pairs={{0,8},{8,16},{16,24},{24,32},{32,40},{40,48},{48,56},{56,64},{64,7... | collective-permute-start | bytes 61448 | tf_op jit(solution)/shard_map/while/body/eval_jaxpr/ppermute | solution.py:10
  130.5 11.7 %collective-permute-start.2 = (f32[32,160]{1,0:T(8,128)S(1)}, f32[32,160]{1,0:T(8,128)S(1)}, u32[]{:S(2)}, u32[]{:S(2)}) collective-permute-start(f32[32,160]{1,0:T(8,128)S(1)} %broadcast_select_fusion.2), channel_id=1, source_target_pairs={{0,8},{8,16},{16,24},{24,32},{32,40},{40,48},{48,56},{56,64},{64,7... | collective-permute-start | bytes 61448 | tf_op jit(solution)/shard_map/while/body/eval_jaxpr/ppermute | solution.py:10
  132.4 9.1 %collective-permute-start.1 = (f32[32,160]{1,0:T(8,128)S(1)}, f32[32,160]{1,0:T(8,128)S(1)}, u32[]{:S(2)}, u32[]{:S(2)}) collective-permute-start(f32[32,160]{1,0:T(8,128)S(1)} %get-tuple-element.160), channel_id=1, source_target_pairs={{0,8},{8,16},{16,24},{24,32},{32,40},{40,48},{48,56},{56,64},{64,7... | collective-permute-start | bytes 61448 | tf_op jit(solution)/shard_map/while/body/eval_jaxpr/ppermute | solution.py:10
  145.0 11.7 %collective-permute-start.2 = (f32[32,160]{1,0:T(8,128)S(1)}, f32[32,160]{1,0:T(8,128)S(1)}, u32[]{:S(2)}, u32[]{:S(2)}) collective-permute-start(f32[32,160]{1,0:T(8,128)S(1)} %broadcast_select_fusion.2), channel_id=1, source_target_pairs={{0,8},{8,16},{16,24},{24,32},{32,40},{40,48},{48,56},{56,64},{64,7... | collective-permute-start | bytes 61448 | tf_op jit(solution)/shard_map/while/body/eval_jaxpr/ppermute | solution.py:10
  146.9 9.1 %collective-permute-start.1 = (f32[32,160]{1,0:T(8,128)S(1)}, f32[32,160]{1,0:T(8,128)S(1)}, u32[]{:S(2)}, u32[]{:S(2)}) collective-permute-start(f32[32,160]{1,0:T(8,128)S(1)} %get-tuple-element.160), channel_id=1, source_target_pairs={{0,8},{8,16},{16,24},{24,32},{32,40},{40,48},{48,56},{56,64},{64,7... | collective-permute-start | bytes 61448 | tf_op jit(solution)/shard_map/while/body/eval_jaxpr/ppermute | solution.py:10
  159.4 11.7 %collective-permute-start.2 = (f32[32,160]{1,0:T(8,128)S(1)}, f32[32,160]{1,0:T(8,128)S(1)}, u32[]{:S(2)}, u32[]{:S(2)}) collective-permute-start(f32[32,160]{1,0:T(8,128)S(1)} %broadcast_select_fusion.2), channel_id=1, source_target_pairs={{0,8},{8,16},{16,24},{24,32},{32,40},{40,48},{48,56},{56,64},{64,7... | collective-permute-start | bytes 61448 | tf_op jit(solution)/shard_map/while/body/eval_jaxpr/ppermute | solution.py:10
  161.4 9.1 %collective-permute-start.1 = (f32[32,160]{1,0:T(8,128)S(1)}, f32[32,160]{1,0:T(8,128)S(1)}, u32[]{:S(2)}, u32[]{:S(2)}) collective-permute-start(f32[32,160]{1,0:T(8,128)S(1)} %get-tuple-element.160), channel_id=1, source_target_pairs={{0,8},{8,16},{16,24},{24,32},{32,40},{40,48},{48,56},{56,64},{64,7... | collective-permute-start | bytes 61448 | tf_op jit(solution)/shard_map/while/body/eval_jaxpr/ppermute | solution.py:10
  173.9 11.7 %collective-permute-start.2 = (f32[32,160]{1,0:T(8,128)S(1)}, f32[32,160]{1,0:T(8,128)S(1)}, u32[]{:S(2)}, u32[]{:S(2)}) collective-permute-start(f32[32,160]{1,0:T(8,128)S(1)} %broadcast_select_fusion.2), channel_id=1, source_target_pairs={{0,8},{8,16},{16,24},{24,32},{32,40},{40,48},{48,56},{56,64},{64,7... | collective-permute-start | bytes 61448 | tf_op jit(solution)/shard_map/while/body/eval_jaxpr/ppermute | solution.py:10
  175.9 9.1 %collective-permute-start.1 = (f32[32,160]{1,0:T(8,128)S(1)}, f32[32,160]{1,0:T(8,128)S(1)}, u32[]{:S(2)}, u32[]{:S(2)}) collective-permute-start(f32[32,160]{1,0:T(8,128)S(1)} %get-tuple-element.160), channel_id=1, source_target_pairs={{0,8},{8,16},{16,24},{24,32},{32,40},{40,48},{48,56},{56,64},{64,7... | collective-permute-start | bytes 61448 | tf_op jit(solution)/shard_map/while/body/eval_jaxpr/ppermute | solution.py:10
  188.4 11.7 %collective-permute-start.2 = (f32[32,160]{1,0:T(8,128)S(1)}, f32[32,160]{1,0:T(8,128)S(1)}, u32[]{:S(2)}, u32[]{:S(2)}) collective-permute-start(f32[32,160]{1,0:T(8,128)S(1)} %broadcast_select_fusion.2), channel_id=1, source_target_pairs={{0,8},{8,16},{16,24},{24,32},{32,40},{40,48},{48,56},{56,64},{64,7... | collective-permute-start | bytes 61448 | tf_op jit(solution)/shard_map/while/body/eval_jaxpr/ppermute | solution.py:10
  190.3 9.1 %collective-permute-start.1 = (f32[32,160]{1,0:T(8,128)S(1)}, f32[32,160]{1,0:T(8,128)S(1)}, u32[]{:S(2)}, u32[]{:S(2)}) collective-permute-start(f32[32,160]{1,0:T(8,128)S(1)} %get-tuple-element.160), channel_id=1, source_target_pairs={{0,8},{8,16},{16,24},{24,32},{32,40},{40,48},{48,56},{56,64},{64,7... | collective-permute-start | bytes 61448 | tf_op jit(solution)/shard_map/while/body/eval_jaxpr/ppermute | solution.py:10
  202.9 11.7 %collective-permute-start.2 = (f32[32,160]{1,0:T(8,128)S(1)}, f32[32,160]{1,0:T(8,128)S(1)}, u32[]{:S(2)}, u32[]{:S(2)}) collective-permute-start(f32[32,160]{1,0:T(8,128)S(1)} %broadcast_select_fusion.2), channel_id=1, source_target_pairs={{0,8},{8,16},{16,24},{24,32},{32,40},{40,48},{48,56},{56,64},{64,7... | collective-permute-start | bytes 61448 | tf_op jit(solution)/shard_map/while/body/eval_jaxpr/ppermute | solution.py:10
  204.8 9.1 %collective-permute-start.1 = (f32[32,160]{1,0:T(8,128)S(1)}, f32[32,160]{1,0:T(8,128)S(1)}, u32[]{:S(2)}, u32[]{:S(2)}) collective-permute-start(f32[32,160]{1,0:T(8,128)S(1)} %get-tuple-element.160), channel_id=1, source_target_pairs={{0,8},{8,16},{16,24},{24,32},{32,40},{40,48},{48,56},{56,64},{64,7... | collective-permute-start | bytes 61448 | tf_op jit(solution)/shard_map/while/body/eval_jaxpr/ppermute | solution.py:10
  217.4 11.7 %collective-permute-start.2 = (f32[32,160]{1,0:T(8,128)S(1)}, f32[32,160]{1,0:T(8,128)S(1)}, u32[]{:S(2)}, u32[]{:S(2)}) collective-permute-start(f32[32,160]{1,0:T(8,128)S(1)} %broadcast_select_fusion.2), channel_id=1, source_target_pairs={{0,8},{8,16},{16,24},{24,32},{32,40},{40,48},{48,56},{56,64},{64,7... | collective-permute-start | bytes 61448 | tf_op jit(solution)/shard_map/while/body/eval_jaxpr/ppermute | solution.py:10
  219.3 9.1 %collective-permute-start.1 = (f32[32,160]{1,0:T(8,128)S(1)}, f32[32,160]{1,0:T(8,128)S(1)}, u32[]{:S(2)}, u32[]{:S(2)}) collective-permute-start(f32[32,160]{1,0:T(8,128)S(1)} %get-tuple-element.160), channel_id=1, source_target_pairs={{0,8},{8,16},{16,24},{24,32},{32,40},{40,48},{48,56},{56,64},{64,7... | collective-permute-start | bytes 61448 | tf_op jit(solution)/shard_map/while/body/eval_jaxpr/ppermute | solution.py:10
  231.9 11.7 %collective-permute-start.2 = (f32[32,160]{1,0:T(8,128)S(1)}, f32[32,160]{1,0:T(8,128)S(1)}, u32[]{:S(2)}, u32[]{:S(2)}) collective-permute-start(f32[32,160]{1,0:T(8,128)S(1)} %broadcast_select_fusion.2), channel_id=1, source_target_pairs={{0,8},{8,16},{16,24},{24,32},{32,40},{40,48},{48,56},{56,64},{64,7... | collective-permute-start | bytes 61448 | tf_op jit(solution)/shard_map/while/body/eval_jaxpr/ppermute | solution.py:10
  233.8 9.1 %collective-permute-start.1 = (f32[32,160]{1,0:T(8,128)S(1)}, f32[32,160]{1,0:T(8,128)S(1)}, u32[]{:S(2)}, u32[]{:S(2)}) collective-permute-start(f32[32,160]{1,0:T(8,128)S(1)} %get-tuple-element.160), channel_id=1, source_target_pairs={{0,8},{8,16},{16,24},{24,32},{32,40},{40,48},{48,56},{56,64},{64,7... | collective-permute-start | bytes 61448 | tf_op jit(solution)/shard_map/while/body/eval_jaxpr/ppermute | solution.py:10
  246.4 11.7 %collective-permute-start.2 = (f32[32,160]{1,0:T(8,128)S(1)}, f32[32,160]{1,0:T(8,128)S(1)}, u32[]{:S(2)}, u32[]{:S(2)}) collective-permute-start(f32[32,160]{1,0:T(8,128)S(1)} %broadcast_select_fusion.2), channel_id=1, source_target_pairs={{0,8},{8,16},{16,24},{24,32},{32,40},{40,48},{48,56},{56,64},{64,7... | collective-permute-start | bytes 61448 | tf_op jit(solution)/shard_map/while/body/eval_jaxpr/ppermute | solution.py:10
  248.3 9.1 %collective-permute-start.1 = (f32[32,160]{1,0:T(8,128)S(1)}, f32[32,160]{1,0:T(8,128)S(1)}, u32[]{:S(2)}, u32[]{:S(2)}) collective-permute-start(f32[32,160]{1,0:T(8,128)S(1)} %get-tuple-element.160), channel_id=1, source_target_pairs={{0,8},{8,16},{16,24},{24,32},{32,40},{40,48},{48,56},{56,64},{64,7... | collective-permute-start | bytes 61448 | tf_op jit(solution)/shard_map/while/body/eval_jaxpr/ppermute | solution.py:10
  260.9 11.7 %collective-permute-start.2 = (f32[32,160]{1,0:T(8,128)S(1)}, f32[32,160]{1,0:T(8,128)S(1)}, u32[]{:S(2)}, u32[]{:S(2)}) collective-permute-start(f32[32,160]{1,0:T(8,128)S(1)} %broadcast_select_fusion.2), channel_id=1, source_target_pairs={{0,8},{8,16},{16,24},{24,32},{32,40},{40,48},{48,56},{56,64},{64,7... | collective-permute-start | bytes 61448 | tf_op jit(solution)/shard_map/while/body/eval_jaxpr/ppermute | solution.py:10
  262.8 9.1 %collective-permute-start.1 = (f32[32,160]{1,0:T(8,128)S(1)}, f32[32,160]{1,0:T(8,128)S(1)}, u32[]{:S(2)}, u32[]{:S(2)}) collective-permute-start(f32[32,160]{1,0:T(8,128)S(1)} %get-tuple-element.160), channel_id=1, source_target_pairs={{0,8},{8,16},{16,24},{24,32},{32,40},{40,48},{48,56},{56,64},{64,7... | collective-permute-start | bytes 61448 | tf_op jit(solution)/shard_map/while/body/eval_jaxpr/ppermute | solution.py:10
  275.3 11.7 %collective-permute-start.2 = (f32[32,160]{1,0:T(8,128)S(1)}, f32[32,160]{1,0:T(8,128)S(1)}, u32[]{:S(2)}, u32[]{:S(2)}) collective-permute-start(f32[32,160]{1,0:T(8,128)S(1)} %broadcast_select_fusion.2), channel_id=1, source_target_pairs={{0,8},{8,16},{16,24},{24,32},{32,40},{40,48},{48,56},{56,64},{64,7... | collective-permute-start | bytes 61448 | tf_op jit(solution)/shard_map/while/body/eval_jaxpr/ppermute | solution.py:10
  277.3 9.1 %collective-permute-start.1 = (f32[32,160]{1,0:T(8,128)S(1)}, f32[32,160]{1,0:T(8,128)S(1)}, u32[]{:S(2)}, u32[]{:S(2)}) collective-permute-start(f32[32,160]{1,0:T(8,128)S(1)} %get-tuple-element.160), channel_id=1, source_target_pairs={{0,8},{8,16},{16,24},{24,32},{32,40},{40,48},{48,56},{56,64},{64,7... | collective-permute-start | bytes 61448 | tf_op jit(solution)/shard_map/while/body/eval_jaxpr/ppermute | solution.py:10
  289.8 11.7 %collective-permute-start.2 = (f32[32,160]{1,0:T(8,128)S(1)}, f32[32,160]{1,0:T(8,128)S(1)}, u32[]{:S(2)}, u32[]{:S(2)}) collective-permute-start(f32[32,160]{1,0:T(8,128)S(1)} %broadcast_select_fusion.2), channel_id=1, source_target_pairs={{0,8},{8,16},{16,24},{24,32},{32,40},{40,48},{48,56},{56,64},{64,7... | collective-permute-start | bytes 61448 | tf_op jit(solution)/shard_map/while/body/eval_jaxpr/ppermute | solution.py:10
  291.8 9.1 %collective-permute-start.1 = (f32[32,160]{1,0:T(8,128)S(1)}, f32[32,160]{1,0:T(8,128)S(1)}, u32[]{:S(2)}, u32[]{:S(2)}) collective-permute-start(f32[32,160]{1,0:T(8,128)S(1)} %get-tuple-element.160), channel_id=1, source_target_pairs={{0,8},{8,16},{16,24},{24,32},{32,40},{40,48},{48,56},{56,64},{64,7... | collective-permute-start | bytes 61448 | tf_op jit(solution)/shard_map/while/body/eval_jaxpr/ppermute | solution.py:10
  304.3 11.7 %collective-permute-start.2 = (f32[32,160]{1,0:T(8,128)S(1)}, f32[32,160]{1,0:T(8,128)S(1)}, u32[]{:S(2)}, u32[]{:S(2)}) collective-permute-start(f32[32,160]{1,0:T(8,128)S(1)} %broadcast_select_fusion.2), channel_id=1, source_target_pairs={{0,8},{8,16},{16,24},{24,32},{32,40},{40,48},{48,56},{56,64},{64,7... | collective-permute-start | bytes 61448 | tf_op jit(solution)/shard_map/while/body/eval_jaxpr/ppermute | solution.py:10
  306.2 9.1 %collective-permute-start.1 = (f32[32,160]{1,0:T(8,128)S(1)}, f32[32,160]{1,0:T(8,128)S(1)}, u32[]{:S(2)}, u32[]{:S(2)}) collective-permute-start(f32[32,160]{1,0:T(8,128)S(1)} %get-tuple-element.160), channel_id=1, source_target_pairs={{0,8},{8,16},{16,24},{24,32},{32,40},{40,48},{48,56},{56,64},{64,7... | collective-permute-start | bytes 61448 | tf_op jit(solution)/shard_map/while/body/eval_jaxpr/ppermute | solution.py:10
  318.8 11.7 %collective-permute-start.2 = (f32[32,160]{1,0:T(8,128)S(1)}, f32[32,160]{1,0:T(8,128)S(1)}, u32[]{:S(2)}, u32[]{:S(2)}) collective-permute-start(f32[32,160]{1,0:T(8,128)S(1)} %broadcast_select_fusion.2), channel_id=1, source_target_pairs={{0,8},{8,16},{16,24},{24,32},{32,40},{40,48},{48,56},{56,64},{64,7... | collective-permute-start | bytes 61448 | tf_op jit(solution)/shard_map/while/body/eval_jaxpr/ppermute | solution.py:10
  320.7 9.1 %collective-permute-start.1 = (f32[32,160]{1,0:T(8,128)S(1)}, f32[32,160]{1,0:T(8,128)S(1)}, u32[]{:S(2)}, u32[]{:S(2)}) collective-permute-start(f32[32,160]{1,0:T(8,128)S(1)} %get-tuple-element.160), channel_id=1, source_target_pairs={{0,8},{8,16},{16,24},{24,32},{32,40},{40,48},{48,56},{56,64},{64,7... | collective-permute-start | bytes 61448 | tf_op jit(solution)/shard_map/while/body/eval_jaxpr/ppermute | solution.py:10
  333.3 11.7 %collective-permute-start.2 = (f32[32,160]{1,0:T(8,128)S(1)}, f32[32,160]{1,0:T(8,128)S(1)}, u32[]{:S(2)}, u32[]{:S(2)}) collective-permute-start(f32[32,160]{1,0:T(8,128)S(1)} %broadcast_select_fusion.2), channel_id=1, source_target_pairs={{0,8},{8,16},{16,24},{24,32},{32,40},{40,48},{48,56},{56,64},{64,7... | collective-permute-start | bytes 61448 | tf_op jit(solution)/shard_map/while/body/eval_jaxpr/ppermute | solution.py:10
  335.2 9.1 %collective-permute-start.1 = (f32[32,160]{1,0:T(8,128)S(1)}, f32[32,160]{1,0:T(8,128)S(1)}, u32[]{:S(2)}, u32[]{:S(2)}) collective-permute-start(f32[32,160]{1,0:T(8,128)S(1)} %get-tuple-element.160), channel_id=1, source_target_pairs={{0,8},{8,16},{16,24},{24,32},{32,40},{40,48},{48,56},{56,64},{64,7... | collective-permute-start | bytes 61448 | tf_op jit(solution)/shard_map/while/body/eval_jaxpr/ppermute | solution.py:10
  347.8 11.7 %collective-permute-start.2 = (f32[32,160]{1,0:T(8,128)S(1)}, f32[32,160]{1,0:T(8,128)S(1)}, u32[]{:S(2)}, u32[]{:S(2)}) collective-permute-start(f32[32,160]{1,0:T(8,128)S(1)} %broadcast_select_fusion.2), channel_id=1, source_target_pairs={{0,8},{8,16},{16,24},{24,32},{32,40},{40,48},{48,56},{56,64},{64,7... | collective-permute-start | bytes 61448 | tf_op jit(solution)/shard_map/while/body/eval_jaxpr/ppermute | solution.py:10
  349.7 9.1 %collective-permute-start.1 = (f32[32,160]{1,0:T(8,128)S(1)}, f32[32,160]{1,0:T(8,128)S(1)}, u32[]{:S(2)}, u32[]{:S(2)}) collective-permute-start(f32[32,160]{1,0:T(8,128)S(1)} %get-tuple-element.160), channel_id=1, source_target_pairs={{0,8},{8,16},{16,24},{24,32},{32,40},{40,48},{48,56},{56,64},{64,7... | collective-permute-start | bytes 61448 | tf_op jit(solution)/shard_map/while/body/eval_jaxpr/ppermute | solution.py:10
  362.3 11.7 %collective-permute-start.2 = (f32[32,160]{1,0:T(8,128)S(1)}, f32[32,160]{1,0:T(8,128)S(1)}, u32[]{:S(2)}, u32[]{:S(2)}) collective-permute-start(f32[32,160]{1,0:T(8,128)S(1)} %broadcast_select_fusion.2), channel_id=1, source_target_pairs={{0,8},{8,16},{16,24},{24,32},{32,40},{40,48},{48,56},{56,64},{64,7... | collective-permute-start | bytes 61448 | tf_op jit(solution)/shard_map/while/body/eval_jaxpr/ppermute | solution.py:10
  364.2 9.1 %collective-permute-start.1 = (f32[32,160]{1,0:T(8,128)S(1)}, f32[32,160]{1,0:T(8,128)S(1)}, u32[]{:S(2)}, u32[]{:S(2)}) collective-permute-start(f32[32,160]{1,0:T(8,128)S(1)} %get-tuple-element.160), channel_id=1, source_target_pairs={{0,8},{8,16},{16,24},{24,32},{32,40},{40,48},{48,56},{56,64},{64,7... | collective-permute-start | bytes 61448 | tf_op jit(solution)/shard_map/while/body/eval_jaxpr/ppermute | solution.py:10
  376.8 11.7 %collective-permute-start.2 = (f32[32,160]{1,0:T(8,128)S(1)}, f32[32,160]{1,0:T(8,128)S(1)}, u32[]{:S(2)}, u32[]{:S(2)}) collective-permute-start(f32[32,160]{1,0:T(8,128)S(1)} %broadcast_select_fusion.2), channel_id=1, source_target_pairs={{0,8},{8,16},{16,24},{24,32},{32,40},{40,48},{48,56},{56,64},{64,7... | collective-permute-start | bytes 61448 | tf_op jit(solution)/shard_map/while/body/eval_jaxpr/ppermute | solution.py:10
  378.7 9.1 %collective-permute-start.1 = (f32[32,160]{1,0:T(8,128)S(1)}, f32[32,160]{1,0:T(8,128)S(1)}, u32[]{:S(2)}, u32[]{:S(2)}) collective-permute-start(f32[32,160]{1,0:T(8,128)S(1)} %get-tuple-element.160), channel_id=1, source_target_pairs={{0,8},{8,16},{16,24},{24,32},{32,40},{40,48},{48,56},{56,64},{64,7... | collective-permute-start | bytes 61448 | tf_op jit(solution)/shard_map/while/body/eval_jaxpr/ppermute | solution.py:10
  391.2 11.7 %collective-permute-start.2 = (f32[32,160]{1,0:T(8,128)S(1)}, f32[32,160]{1,0:T(8,128)S(1)}, u32[]{:S(2)}, u32[]{:S(2)}) collective-permute-start(f32[32,160]{1,0:T(8,128)S(1)} %broadcast_select_fusion.2), channel_id=1, source_target_pairs={{0,8},{8,16},{16,24},{24,32},{32,40},{40,48},{48,56},{56,64},{64,7... | collective-permute-start | bytes 61448 | tf_op jit(solution)/shard_map/while/body/eval_jaxpr/ppermute | solution.py:10
  393.2 9.1 %collective-permute-start.1 = (f32[32,160]{1,0:T(8,128)S(1)}, f32[32,160]{1,0:T(8,128)S(1)}, u32[]{:S(2)}, u32[]{:S(2)}) collective-permute-start(f32[32,160]{1,0:T(8,128)S(1)} %get-tuple-element.160), channel_id=1, source_target_pairs={{0,8},{8,16},{16,24},{24,32},{32,40},{40,48},{48,56},{56,64},{64,7... | collective-permute-start | bytes 61448 | tf_op jit(solution)/shard_map/while/body/eval_jaxpr/ppermute | solution.py:10
  405.7 11.7 %collective-permute-start.2 = (f32[32,160]{1,0:T(8,128)S(1)}, f32[32,160]{1,0:T(8,128)S(1)}, u32[]{:S(2)}, u32[]{:S(2)}) collective-permute-start(f32[32,160]{1,0:T(8,128)S(1)} %broadcast_select_fusion.2), channel_id=1, source_target_pairs={{0,8},{8,16},{16,24},{24,32},{32,40},{40,48},{48,56},{56,64},{64,7... | collective-permute-start | bytes 61448 | tf_op jit(solution)/shard_map/while/body/eval_jaxpr/ppermute | solution.py:10
  407.7 9.1 %collective-permute-start.1 = (f32[32,160]{1,0:T(8,128)S(1)}, f32[32,160]{1,0:T(8,128)S(1)}, u32[]{:S(2)}, u32[]{:S(2)}) collective-permute-start(f32[32,160]{1,0:T(8,128)S(1)} %get-tuple-element.160), channel_id=1, source_target_pairs={{0,8},{8,16},{16,24},{24,32},{32,40},{40,48},{48,56},{56,64},{64,7... | collective-permute-start | bytes 61448 | tf_op jit(solution)/shard_map/while/body/eval_jaxpr/ppermute | solution.py:10
  420.2 11.7 %collective-permute-start.2 = (f32[32,160]{1,0:T(8,128)S(1)}, f32[32,160]{1,0:T(8,128)S(1)}, u32[]{:S(2)}, u32[]{:S(2)}) collective-permute-start(f32[32,160]{1,0:T(8,128)S(1)} %broadcast_select_fusion.2), channel_id=1, source_target_pairs={{0,8},{8,16},{16,24},{24,32},{32,40},{40,48},{48,56},{56,64},{64,7... | collective-permute-start | bytes 61448 | tf_op jit(solution)/shard_map/while/body/eval_jaxpr/ppermute | solution.py:10
  422.1 9.1 %collective-permute-start.1 = (f32[32,160]{1,0:T(8,128)S(1)}, f32[32,160]{1,0:T(8,128)S(1)}, u32[]{:S(2)}, u32[]{:S(2)}) collective-permute-start(f32[32,160]{1,0:T(8,128)S(1)} %get-tuple-element.160), channel_id=1, source_target_pairs={{0,8},{8,16},{16,24},{24,32},{32,40},{40,48},{48,56},{56,64},{64,7... | collective-permute-start | bytes 61448 | tf_op jit(solution)/shard_map/while/body/eval_jaxpr/ppermute | solution.py:10
  434.7 11.7 %collective-permute-start.2 = (f32[32,160]{1,0:T(8,128)S(1)}, f32[32,160]{1,0:T(8,128)S(1)}, u32[]{:S(2)}, u32[]{:S(2)}) collective-permute-start(f32[32,160]{1,0:T(8,128)S(1)} %broadcast_select_fusion.2), channel_id=1, source_target_pairs={{0,8},{8,16},{16,24},{24,32},{32,40},{40,48},{48,56},{56,64},{64,7... | collective-permute-start | bytes 61448 | tf_op jit(solution)/shard_map/while/body/eval_jaxpr/ppermute | solution.py:10
  436.6 9.1 %collective-permute-start.1 = (f32[32,160]{1,0:T(8,128)S(1)}, f32[32,160]{1,0:T(8,128)S(1)}, u32[]{:S(2)}, u32[]{:S(2)}) collective-permute-start(f32[32,160]{1,0:T(8,128)S(1)} %get-tuple-element.160), channel_id=1, source_target_pairs={{0,8},{8,16},{16,24},{24,32},{32,40},{40,48},{48,56},{56,64},{64,7... | collective-permute-start | bytes 61448 | tf_op jit(solution)/shard_map/while/body/eval_jaxpr/ppermute | solution.py:10
  449.2 11.7 %collective-permute-start.2 = (f32[32,160]{1,0:T(8,128)S(1)}, f32[32,160]{1,0:T(8,128)S(1)}, u32[]{:S(2)}, u32[]{:S(2)}) collective-permute-start(f32[32,160]{1,0:T(8,128)S(1)} %broadcast_select_fusion.2), channel_id=1, source_target_pairs={{0,8},{8,16},{16,24},{24,32},{32,40},{40,48},{48,56},{56,64},{64,7... | collective-permute-start | bytes 61448 | tf_op jit(solution)/shard_map/while/body/eval_jaxpr/ppermute | solution.py:10
  463.7 11.7 %collective-permute-start.2 = (f32[32,160]{1,0:T(8,128)S(1)}, f32[32,160]{1,0:T(8,128)S(1)}, u32[]{:S(2)}, u32[]{:S(2)}) collective-permute-start(f32[32,160]{1,0:T(8,128)S(1)} %broadcast_select_fusion.2), channel_id=1, source_target_pairs={{0,8},{8,16},{16,24},{24,32},{32,40},{40,48},{48,56},{56,64},{64,7... | collective-permute-start | bytes 61448 | tf_op jit(solution)/shard_map/while/body/eval_jaxpr/ppermute | solution.py:10
  465.6 9.1 %collective-permute-start.1 = (f32[32,160]{1,0:T(8,128)S(1)}, f32[32,160]{1,0:T(8,128)S(1)}, u32[]{:S(2)}, u32[]{:S(2)}) collective-permute-start(f32[32,160]{1,0:T(8,128)S(1)} %get-tuple-element.160), channel_id=1, source_target_pairs={{0,8},{8,16},{16,24},{24,32},{32,40},{40,48},{48,56},{56,64},{64,7... | collective-permute-start | bytes 61448 | tf_op jit(solution)/shard_map/while/body/eval_jaxpr/ppermute | solution.py:10
  478.2 11.7 %collective-permute-start.2 = (f32[32,160]{1,0:T(8,128)S(1)}, f32[32,160]{1,0:T(8,128)S(1)}, u32[]{:S(2)}, u32[]{:S(2)}) collective-permute-start(f32[32,160]{1,0:T(8,128)S(1)} %broadcast_select_fusion.2), channel_id=1, source_target_pairs={{0,8},{8,16},{16,24},{24,32},{32,40},{40,48},{48,56},{56,64},{64,7... | collective-permute-start | bytes 61448 | tf_op jit(solution)/shard_map/while/body/eval_jaxpr/ppermute | solution.py:10
  480.1 9.1 %collective-permute-start.1 = (f32[32,160]{1,0:T(8,128)S(1)}, f32[32,160]{1,0:T(8,128)S(1)}, u32[]{:S(2)}, u32[]{:S(2)}) collective-permute-start(f32[32,160]{1,0:T(8,128)S(1)} %get-tuple-element.160), channel_id=1, source_target_pairs={{0,8},{8,16},{16,24},{24,32},{32,40},{40,48},{48,56},{56,64},{64,7... | collective-permute-start | bytes 61448 | tf_op jit(solution)/shard_map/while/body/eval_jaxpr/ppermute | solution.py:10
  492.7 11.7 %collective-permute-start.2 = (f32[32,160]{1,0:T(8,128)S(1)}, f32[32,160]{1,0:T(8,128)S(1)}, u32[]{:S(2)}, u32[]{:S(2)}) collective-permute-start(f32[32,160]{1,0:T(8,128)S(1)} %broadcast_select_fusion.2), channel_id=1, source_target_pairs={{0,8},{8,16},{16,24},{24,32},{32,40},{40,48},{48,56},{56,64},{64,7... | collective-permute-start | bytes 61448 | tf_op jit(solution)/shard_map/while/body/eval_jaxpr/ppermute | solution.py:10
  494.6 9.1 %collective-permute-start.1 = (f32[32,160]{1,0:T(8,128)S(1)}, f32[32,160]{1,0:T(8,128)S(1)}, u32[]{:S(2)}, u32[]{:S(2)}) collective-permute-start(f32[32,160]{1,0:T(8,128)S(1)} %get-tuple-element.160), channel_id=1, source_target_pairs={{0,8},{8,16},{16,24},{24,32},{32,40},{40,48},{48,56},{56,64},{64,7... | collective-permute-start | bytes 61448 | tf_op jit(solution)/shard_map/while/body/eval_jaxpr/ppermute | solution.py:10
  507.1 11.7 %collective-permute-start.2 = (f32[32,160]{1,0:T(8,128)S(1)}, f32[32,160]{1,0:T(8,128)S(1)}, u32[]{:S(2)}, u32[]{:S(2)}) collective-permute-start(f32[32,160]{1,0:T(8,128)S(1)} %broadcast_select_fusion.2), channel_id=1, source_target_pairs={{0,8},{8,16},{16,24},{24,32},{32,40},{40,48},{48,56},{56,64},{64,7... | collective-permute-start | bytes 61448 | tf_op jit(solution)/shard_map/while/body/eval_jaxpr/ppermute | solution.py:10
  509.1 9.1 %collective-permute-start.1 = (f32[32,160]{1,0:T(8,128)S(1)}, f32[32,160]{1,0:T(8,128)S(1)}, u32[]{:S(2)}, u32[]{:S(2)}) collective-permute-start(f32[32,160]{1,0:T(8,128)S(1)} %get-tuple-element.160), channel_id=1, source_target_pairs={{0,8},{8,16},{16,24},{24,32},{32,40},{40,48},{48,56},{56,64},{64,7... | collective-permute-start | bytes 61448 | tf_op jit(solution)/shard_map/while/body/eval_jaxpr/ppermute | solution.py:10
  521.6 11.7 %collective-permute-start.2 = (f32[32,160]{1,0:T(8,128)S(1)}, f32[32,160]{1,0:T(8,128)S(1)}, u32[]{:S(2)}, u32[]{:S(2)}) collective-permute-start(f32[32,160]{1,0:T(8,128)S(1)} %broadcast_select_fusion.2), channel_id=1, source_target_pairs={{0,8},{8,16},{16,24},{24,32},{32,40},{40,48},{48,56},{56,64},{64,7... | collective-permute-start | bytes 61448 | tf_op jit(solution)/shard_map/while/body/eval_jaxpr/ppermute | solution.py:10
  523.6 9.1 %collective-permute-start.1 = (f32[32,160]{1,0:T(8,128)S(1)}, f32[32,160]{1,0:T(8,128)S(1)}, u32[]{:S(2)}, u32[]{:S(2)}) collective-permute-start(f32[32,160]{1,0:T(8,128)S(1)} %get-tuple-element.160), channel_id=1, source_target_pairs={{0,8},{8,16},{16,24},{24,32},{32,40},{40,48},{48,56},{56,64},{64,7... | collective-permute-start | bytes 61448 | tf_op jit(solution)/shard_map/while/body/eval_jaxpr/ppermute | solution.py:10
  536.1 11.7 %collective-permute-start.2 = (f32[32,160]{1,0:T(8,128)S(1)}, f32[32,160]{1,0:T(8,128)S(1)}, u32[]{:S(2)}, u32[]{:S(2)}) collective-permute-start(f32[32,160]{1,0:T(8,128)S(1)} %broadcast_select_fusion.2), channel_id=1, source_target_pairs={{0,8},{8,16},{16,24},{24,32},{32,40},{40,48},{48,56},{56,64},{64,7... | collective-permute-start | bytes 61448 | tf_op jit(solution)/shard_map/while/body/eval_jaxpr/ppermute | solution.py:10
  538.0 9.1 %collective-permute-start.1 = (f32[32,160]{1,0:T(8,128)S(1)}, f32[32,160]{1,0:T(8,128)S(1)}, u32[]{:S(2)}, u32[]{:S(2)}) collective-permute-start(f32[32,160]{1,0:T(8,128)S(1)} %get-tuple-element.160), channel_id=1, source_target_pairs={{0,8},{8,16},{16,24},{24,32},{32,40},{40,48},{48,56},{56,64},{64,7... | collective-permute-start | bytes 61448 | tf_op jit(solution)/shard_map/while/body/eval_jaxpr/ppermute | solution.py:10
  550.6 9.4 %collective-permute-start.3 = (f32[32,160]{1,0:T(8,128)S(1)}, f32[32,160]{1,0:T(8,128)S(1)}, u32[]{:S(2)}, u32[]{:S(2)}) collective-permute-start(f32[32,160]{1,0:T(8,128)S(1)} %get-tuple-element.51), channel_id=1, source_target_pairs={{0,8},{8,16},{16,24},{24,32},{32,40},{40,48},{48,56},{56,64},{64,7... | collective-permute-start | bytes 61448 | tf_op jit(solution)/shard_map/ppermute | solution.py:10
  562.3 94.8 %collective-permute-start.5 = (f32[32,160]{1,0:T(8,128)S(1)}, f32[32,160]{1,0:T(8,128)S(1)}, u32[]{:S(2)}, u32[]{:S(2)}) collective-permute-start(f32[32,160]{1,0:T(8,128)S(1)} %get-tuple-element.53), channel_id=1, source_target_pairs={{0,264},{8,272},{16,280},{24,288},{32,296},{40,304},{48,312},{56,3... | collective-permute-start | bytes 61448 | tf_op jit(solution)/shard_map/ppermute | solution.py:10
  (35 other events, 297.5 us)
Sparse Core Ops, SparseCore 0:
  562.4 93.7 reduce-scatter.3
where the time goes:
time: 668 us; the launch traced here: 665 us
  waiting for transfers between devices  280 us (42%)
  starting transfers between devices  187 us (28%)
  blocking collectives  88.4 us (13%)
  matrix products  86.7 us (13%)
  between operations  13.5 us (2%)
    ppermute x96, waiting for transfers between devices, shifted(): return lax.ppermute(value, axis, pairs)  190 us
    ppermute x96, starting transfers between devices, shifted(): return lax.ppermute(value, axis, pairs)  187 us
    unnamed x2, waiting for transfers between devices  89.7 us
    all_gather x1, blocking collectives, per_device(): lax.all_gather(local_z, 'rep', axis=1, tiled=True)  44.3 us
    all_gather x1, blocking collectives, per_device(): lax.all_gather(vectors, 'rep', axis=1, tiled=True)  44 us
    dot_general x33, matrix products, matern_tile(): lax.dot_general(col_z, row_z, (((0,), (0,)), ((), ())), precision=lax.Pre...  40.8 us
    dot_general x31, matrix products, cols_times(): lax.dot_general(row_v, kernel, (((1,), (1,)), ((), ())), precision=lax.Pr...  26.3 us
    dot_general x33, matrix products, rows_times(): lax.dot(col_v, kernel, precision=lax.Precision.HIGHEST, preferred_element...  19.6 us
  transfers between devices with their start and end apart: 97, of which 65 were waited for; matrix products, arithmetic and copies ran while one was open for 9% of the time, Pallas kernels for 0%

commit v1 on v0

--- a/solution.py
+++ b/solution.py
@@ -42,10 +42,14 @@
 
 def per_device(points, vectors, lengthscales):
     local_z = points / lengthscales[:, None]
-    row_z, row_v = (
-        lax.all_gather(local_z, "rep", axis=1, tiled=True),
-        lax.all_gather(vectors, "rep", axis=1, tiled=True),
-    )
+
+    def refer_indices(z_in):
+        low = jax.lax.axis_size("rep")
+        v_now = jnp.stack(low * [z_in])
+        tile_out = jax.lax.all_to_all(v_now, axis_name="rep", split_axis=0, concat_axis=0)
+        return jnp.concatenate(tile_out, axis=1)
+
+    row_z, row_v = (refer_indices(local_z), lax.all_gather(vectors, "rep", axis=1, tiled=True))
     row_sq = jnp.sum(row_z * row_z, axis=0)
     half = lax.axis_size("blk") // 2
     row_acc = rows_times(vectors, matern_tile(local_z, row_z, row_sq))

time: 668 us -> 633 us (0.948)
  blocking collectives: 88.4 us -> 44.1 us
  starting transfers between devices: 187 us -> 197 us
    all_gather x1 -> x0, blocking collectives: 44.3 us -> none  [per_device(): lax.all_gather(local_z, 'rep', axis=1, tiled=True)]
    all_to_all x0 -> x1, starting transfers between devices: none -> 10.1 us  [refer_indices(): jax.lax.all_to_all(v_now, axis_name='rep', split_axis=0, concat_axis=0)]
  transfers between devices with their start and end apart: 97 -> 98, of which waited for: 65 -> 65; matrix products, arithmetic and copies ran while one was open for 9% -> 9% of each run, Pallas kernels for 0% -> 0%
where the time goes in v1:
time: 633 us; the launch traced here: 630 us
  waiting for transfers between devices  280 us (44%)
  starting transfers between devices  197 us (31%)
  matrix products  86.7 us (14%)
  blocking collectives  44.1 us (7%)
  between operations  13.5 us (2%)
    ppermute x96, waiting for transfers between devices, shifted(): return lax.ppermute(value, axis, pairs)  190 us
    ppermute x96, starting transfers between devices, shifted(): return lax.ppermute(value, axis, pairs)  187 us
    unnamed x2, waiting for transfers between devices  89.5 us
    all_gather x1, blocking collectives, per_device(): lax.all_gather(vectors, 'rep', axis=1, tiled=True)  44.1 us
    dot_general x33, matrix products, matern_tile(): lax.dot_general(col_z, row_z, (((0,), (0,)), ((), ())), precision=lax.Pre...  40.9 us
    dot_general x31, matrix products, cols_times(): lax.dot_general(row_v, kernel, (((1,), (1,)), ((), ())), precision=lax.Pr...  26.3 us
    dot_general x33, matrix products, rows_times(): lax.dot(col_v, kernel, precision=lax.Precision.HIGHEST, preferred_element...  19.6 us
  transfers between devices with their start and end apart: 98, of which 65 were waited for; matrix products, arithmetic and copies ran while one was open for 9% of the time, Pallas kernels for 0%

profile of v1, /device:TPU:2, one launch (start us, length us, event | category | flops | bytes accessed | tf_op | source)
XLA Modules:
  0.0 630.3 jit_solution(4819993507204555412)
XLA Ops:
  8.1 10.1 %all-to-all-start = ((f32[8,16,160]{2,1,0:T(8,128)}), f32[8,16,160]{2,1,0:T(8,128)S(1)}, u32[]{:S(2)}, u32[]{:S(2)}) async-start(f32[8,16,160]{2,1,0:T(8,128)} %stack.2), calls=%async_computation | async-start | bytes 262144 | tf_op jit(solution)/shard_map/all_to_all | solution.py:49
  18.2 44.1 %all-gather = f32[8,160,32]{1,2,0:T(8,128)S(1)} all-gather(f32[1,160,32]{1,2,0:T(8,128)S(1)} %bitcast.51), channel_id=1, replica_groups=mesh['blk'=64,'rep'=8] {'rep'}, dimensions={0}, use_global_device_ids=true | all-gather | bytes 184320 | tf_op jit(solution)/shard_map/all_gather | solution.py:52
  64.7 449.9 %while.17 = (s32[]{:T(128)}, f32[16,160]{1,0:T(8,128)S(1)}, f32[32,160]{1,0:T(8,128)S(1)}, f32[32,160]{1,0:T(8,128)S(1)}, f32[32,1280]{1,0:T(8,128)S(1)}, /*inde...) while((s32[]{:T(128)}, f32[16,160]{1,0:T(8,128)S(1)}, ...), condition=%wide.region_4.0_spmd.clone, body=%wide.region_2.0_spmd.clone.sunk | while | flops 198916960 | bytes 3426791 | solution.py:69
  75.0 3.5 collective-permute-done.1
  85.7 3.2 collective-permute-done
  90.2 2.8 collective-permute-done.1
  100.2 3.2 collective-permute-done
  104.7 2.8 collective-permute-done.1
  114.7 3.2 collective-permute-done
  119.2 2.8 collective-permute-done.1
  129.2 3.2 collective-permute-done
  133.7 2.8 collective-permute-done.1
  143.7 3.2 collective-permute-done
  148.1 2.8 collective-permute-done.1
  158.2 3.2 collective-permute-done
  162.6 2.8 collective-permute-done.1
  172.7 3.2 collective-permute-done
  177.1 2.8 collective-permute-done.1
  187.1 3.2 collective-permute-done
  191.6 2.8 collective-permute-done.1
  201.6 3.2 collective-permute-done
  206.1 2.8 collective-permute-done.1
  216.1 3.2 collective-permute-done
  220.6 2.8 collective-permute-done.1
  230.6 3.2 collective-permute-done
  235.1 2.8 collective-permute-done.1
  245.1 3.2 collective-permute-done
  249.5 2.8 collective-permute-done.1
  259.6 3.2 collective-permute-done
  264.0 2.8 collective-permute-done.1
  274.1 3.2 collective-permute-done
  278.5 2.8 collective-permute-done.1
  288.6 3.2 collective-permute-done
  293.0 2.8 collective-permute-done.1
  303.0 3.2 collective-permute-done
  307.5 2.8 collective-permute-done.1
  317.5 3.2 collective-permute-done
  322.0 2.8 collective-permute-done.1
  332.0 3.2 collective-permute-done
  336.5 2.8 collective-permute-done.1
  346.5 3.2 collective-permute-done
  351.0 2.8 collective-permute-done.1
  361.0 3.2 collective-permute-done
  365.4 2.8 collective-permute-done.1
  375.5 3.2 collective-permute-done
  379.9 2.8 collective-permute-done.1
  390.0 3.2 collective-permute-done
  394.4 2.8 collective-permute-done.1
  404.5 3.2 collective-permute-done
  408.9 2.8 collective-permute-done.1
  418.9 3.2 collective-permute-done
  423.4 2.8 collective-permute-done.1
  433.4 3.2 collective-permute-done
  437.9 2.8 collective-permute-done.1
  447.9 3.2 collective-permute-done
  462.4 3.2 collective-permute-done
  466.9 2.8 collective-permute-done.1
  476.9 3.2 collective-permute-done
  491.4 3.2 collective-permute-done
  505.9 3.2 collective-permute-done
  510.3 2.8 collective-permute-done.1
  518.4 5.1 collective-permute-done.4
  528.2 4.2 collective-permute-start.5
  532.4 89.5 %reduce-scatter.4.cloned.1.call-done = f32[160,32]{1,0:T(8,128)} async-done(((f32[1280,32]{1,0:T(8,128)}), f32[160,32]{1,0:T(8,128)}) %reduce-scatter.4.cloned.1.call-update) | async-done | bytes 20496
  (374 shorter events, 288.1 us)
Async XLA Ops:
  8.1 54.5 %all-to-all-start = ((f32[8,16,160]{2,1,0:T(8,128)}), f32[8,16,160]{2,1,0:T(8,128)S(1)}, u32[]{:S(2)}, u32[]{:S(2)}) async-start(f32[8,16,160]{2,1,0:T(8,128)} %stack.2), calls=%async_computation | async-start | bytes 262144 | tf_op jit(solution)/shard_map/all_to_all | solution.py:49
  18.2 603.7 %reduce-scatter.4.cloned.1.call-start = ((), (), s32[]{:S(2)}) async-start(), calls=%async_computation.2 | async-start | bytes 737280
  66.6 12.4 %collective-permute-start.2 = (f32[32,160]{1,0:T(8,128)S(1)}, f32[32,160]{1,0:T(8,128)S(1)}, u32[]{:S(2)}, u32[]{:S(2)}) collective-permute-start(f32[32,160]{1,0:T(8,128)S(1)} %broadcast_select_fusion.2), channel_id=1, source_target_pairs={{0,8},{8,16},{16,24},{24,32},{32,40},{40,48},{48,56},{56,64},{64,7... | collective-permute-start | bytes 61448 | tf_op jit(solution)/shard_map/while/body/eval_jaxpr/ppermute | solution.py:10
  69.3 9.1 %collective-permute-start.1 = (f32[32,160]{1,0:T(8,128)S(1)}, f32[32,160]{1,0:T(8,128)S(1)}, u32[]{:S(2)}, u32[]{:S(2)}) collective-permute-start(f32[32,160]{1,0:T(8,128)S(1)} %get-tuple-element.160), channel_id=1, source_target_pairs={{0,8},{8,16},{16,24},{24,32},{32,40},{40,48},{48,56},{56,64},{64,7... | collective-permute-start | bytes 61448 | tf_op jit(solution)/shard_map/while/body/eval_jaxpr/ppermute | solution.py:10
  81.9 11.7 %collective-permute-start.2 = (f32[32,160]{1,0:T(8,128)S(1)}, f32[32,160]{1,0:T(8,128)S(1)}, u32[]{:S(2)}, u32[]{:S(2)}) collective-permute-start(f32[32,160]{1,0:T(8,128)S(1)} %broadcast_select_fusion.2), channel_id=1, source_target_pairs={{0,8},{8,16},{16,24},{24,32},{32,40},{40,48},{48,56},{56,64},{64,7... | collective-permute-start | bytes 61448 | tf_op jit(solution)/shard_map/while/body/eval_jaxpr/ppermute | solution.py:10
  83.8 9.1 %collective-permute-start.1 = (f32[32,160]{1,0:T(8,128)S(1)}, f32[32,160]{1,0:T(8,128)S(1)}, u32[]{:S(2)}, u32[]{:S(2)}) collective-permute-start(f32[32,160]{1,0:T(8,128)S(1)} %get-tuple-element.160), channel_id=1, source_target_pairs={{0,8},{8,16},{16,24},{24,32},{32,40},{40,48},{48,56},{56,64},{64,7... | collective-permute-start | bytes 61448 | tf_op jit(solution)/shard_map/while/body/eval_jaxpr/ppermute | solution.py:10
  96.4 11.7 %collective-permute-start.2 = (f32[32,160]{1,0:T(8,128)S(1)}, f32[32,160]{1,0:T(8,128)S(1)}, u32[]{:S(2)}, u32[]{:S(2)}) collective-permute-start(f32[32,160]{1,0:T(8,128)S(1)} %broadcast_select_fusion.2), channel_id=1, source_target_pairs={{0,8},{8,16},{16,24},{24,32},{32,40},{40,48},{48,56},{56,64},{64,7... | collective-permute-start | bytes 61448 | tf_op jit(solution)/shard_map/while/body/eval_jaxpr/ppermute | solution.py:10
  98.3 9.1 %collective-permute-start.1 = (f32[32,160]{1,0:T(8,128)S(1)}, f32[32,160]{1,0:T(8,128)S(1)}, u32[]{:S(2)}, u32[]{:S(2)}) collective-permute-start(f32[32,160]{1,0:T(8,128)S(1)} %get-tuple-element.160), channel_id=1, source_target_pairs={{0,8},{8,16},{16,24},{24,32},{32,40},{40,48},{48,56},{56,64},{64,7... | collective-permute-start | bytes 61448 | tf_op jit(solution)/shard_map/while/body/eval_jaxpr/ppermute | solution.py:10
  110.8 11.7 %collective-permute-start.2 = (f32[32,160]{1,0:T(8,128)S(1)}, f32[32,160]{1,0:T(8,128)S(1)}, u32[]{:S(2)}, u32[]{:S(2)}) collective-permute-start(f32[32,160]{1,0:T(8,128)S(1)} %broadcast_select_fusion.2), channel_id=1, source_target_pairs={{0,8},{8,16},{16,24},{24,32},{32,40},{40,48},{48,56},{56,64},{64,7... | collective-permute-start | bytes 61448 | tf_op jit(solution)/shard_map/while/body/eval_jaxpr/ppermute | solution.py:10
  112.8 9.1 %collective-permute-start.1 = (f32[32,160]{1,0:T(8,128)S(1)}, f32[32,160]{1,0:T(8,128)S(1)}, u32[]{:S(2)}, u32[]{:S(2)}) collective-permute-start(f32[32,160]{1,0:T(8,128)S(1)} %get-tuple-element.160), channel_id=1, source_target_pairs={{0,8},{8,16},{16,24},{24,32},{32,40},{40,48},{48,56},{56,64},{64,7... | collective-permute-start | bytes 61448 | tf_op jit(solution)/shard_map/while/body/eval_jaxpr/ppermute | solution.py:10
  125.3 11.7 %collective-permute-start.2 = (f32[32,160]{1,0:T(8,128)S(1)}, f32[32,160]{1,0:T(8,128)S(1)}, u32[]{:S(2)}, u32[]{:S(2)}) collective-permute-start(f32[32,160]{1,0:T(8,128)S(1)} %broadcast_select_fusion.2), channel_id=1, source_target_pairs={{0,8},{8,16},{16,24},{24,32},{32,40},{40,48},{48,56},{56,64},{64,7... | collective-permute-start | bytes 61448 | tf_op jit(solution)/shard_map/while/body/eval_jaxpr/ppermute | solution.py:10
  127.3 9.1 %collective-permute-start.1 = (f32[32,160]{1,0:T(8,128)S(1)}, f32[32,160]{1,0:T(8,128)S(1)}, u32[]{:S(2)}, u32[]{:S(2)}) collective-permute-start(f32[32,160]{1,0:T(8,128)S(1)} %get-tuple-element.160), channel_id=1, source_target_pairs={{0,8},{8,16},{16,24},{24,32},{32,40},{40,48},{48,56},{56,64},{64,7... | collective-permute-start | bytes 61448 | tf_op jit(solution)/shard_map/while/body/eval_jaxpr/ppermute | solution.py:10
  139.8 11.7 %collective-permute-start.2 = (f32[32,160]{1,0:T(8,128)S(1)}, f32[32,160]{1,0:T(8,128)S(1)}, u32[]{:S(2)}, u32[]{:S(2)}) collective-permute-start(f32[32,160]{1,0:T(8,128)S(1)} %broadcast_select_fusion.2), channel_id=1, source_target_pairs={{0,8},{8,16},{16,24},{24,32},{32,40},{40,48},{48,56},{56,64},{64,7... | collective-permute-start | bytes 61448 | tf_op jit(solution)/shard_map/while/body/eval_jaxpr/ppermute | solution.py:10
  141.8 9.1 %collective-permute-start.1 = (f32[32,160]{1,0:T(8,128)S(1)}, f32[32,160]{1,0:T(8,128)S(1)}, u32[]{:S(2)}, u32[]{:S(2)}) collective-permute-start(f32[32,160]{1,0:T(8,128)S(1)} %get-tuple-element.160), channel_id=1, source_target_pairs={{0,8},{8,16},{16,24},{24,32},{32,40},{40,48},{48,56},{56,64},{64,7... | collective-permute-start | bytes 61448 | tf_op jit(solution)/shard_map/while/body/eval_jaxpr/ppermute | solution.py:10
  154.3 11.7 %collective-permute-start.2 = (f32[32,160]{1,0:T(8,128)S(1)}, f32[32,160]{1,0:T(8,128)S(1)}, u32[]{:S(2)}, u32[]{:S(2)}) collective-permute-start(f32[32,160]{1,0:T(8,128)S(1)} %broadcast_select_fusion.2), channel_id=1, source_target_pairs={{0,8},{8,16},{16,24},{24,32},{32,40},{40,48},{48,56},{56,64},{64,7... | collective-permute-start | bytes 61448 | tf_op jit(solution)/shard_map/while/body/eval_jaxpr/ppermute | solution.py:10
  156.2 9.1 %collective-permute-start.1 = (f32[32,160]{1,0:T(8,128)S(1)}, f32[32,160]{1,0:T(8,128)S(1)}, u32[]{:S(2)}, u32[]{:S(2)}) collective-permute-start(f32[32,160]{1,0:T(8,128)S(1)} %get-tuple-element.160), channel_id=1, source_target_pairs={{0,8},{8,16},{16,24},{24,32},{32,40},{40,48},{48,56},{56,64},{64,7... | collective-permute-start | bytes 61448 | tf_op jit(solution)/shard_map/while/body/eval_jaxpr/ppermute | solution.py:10
  168.8 11.7 %collective-permute-start.2 = (f32[32,160]{1,0:T(8,128)S(1)}, f32[32,160]{1,0:T(8,128)S(1)}, u32[]{:S(2)}, u32[]{:S(2)}) collective-permute-start(f32[32,160]{1,0:T(8,128)S(1)} %broadcast_select_fusion.2), channel_id=1, source_target_pairs={{0,8},{8,16},{16,24},{24,32},{32,40},{40,48},{48,56},{56,64},{64,7... | collective-permute-start | bytes 61448 | tf_op jit(solution)/shard_map/while/body/eval_jaxpr/ppermute | solution.py:10
  170.7 9.1 %collective-permute-start.1 = (f32[32,160]{1,0:T(8,128)S(1)}, f32[32,160]{1,0:T(8,128)S(1)}, u32[]{:S(2)}, u32[]{:S(2)}) collective-permute-start(f32[32,160]{1,0:T(8,128)S(1)} %get-tuple-element.160), channel_id=1, source_target_pairs={{0,8},{8,16},{16,24},{24,32},{32,40},{40,48},{48,56},{56,64},{64,7... | collective-permute-start | bytes 61448 | tf_op jit(solution)/shard_map/while/body/eval_jaxpr/ppermute | solution.py:10
  183.3 11.7 %collective-permute-start.2 = (f32[32,160]{1,0:T(8,128)S(1)}, f32[32,160]{1,0:T(8,128)S(1)}, u32[]{:S(2)}, u32[]{:S(2)}) collective-permute-start(f32[32,160]{1,0:T(8,128)S(1)} %broadcast_select_fusion.2), channel_id=1, source_target_pairs={{0,8},{8,16},{16,24},{24,32},{32,40},{40,48},{48,56},{56,64},{64,7... | collective-permute-start | bytes 61448 | tf_op jit(solution)/shard_map/while/body/eval_jaxpr/ppermute | solution.py:10
  185.2 9.1 %collective-permute-start.1 = (f32[32,160]{1,0:T(8,128)S(1)}, f32[32,160]{1,0:T(8,128)S(1)}, u32[]{:S(2)}, u32[]{:S(2)}) collective-permute-start(f32[32,160]{1,0:T(8,128)S(1)} %get-tuple-element.160), channel_id=1, source_target_pairs={{0,8},{8,16},{16,24},{24,32},{32,40},{40,48},{48,56},{56,64},{64,7... | collective-permute-start | bytes 61448 | tf_op jit(solution)/shard_map/while/body/eval_jaxpr/ppermute | solution.py:10
  197.8 11.7 %collective-permute-start.2 = (f32[32,160]{1,0:T(8,128)S(1)}, f32[32,160]{1,0:T(8,128)S(1)}, u32[]{:S(2)}, u32[]{:S(2)}) collective-permute-start(f32[32,160]{1,0:T(8,128)S(1)} %broadcast_select_fusion.2), channel_id=1, source_target_pairs={{0,8},{8,16},{16,24},{24,32},{32,40},{40,48},{48,56},{56,64},{64,7... | collective-permute-start | bytes 61448 | tf_op jit(solution)/shard_map/while/body/eval_jaxpr/ppermute | solution.py:10
  199.7 9.1 %collective-permute-start.1 = (f32[32,160]{1,0:T(8,128)S(1)}, f32[32,160]{1,0:T(8,128)S(1)}, u32[]{:S(2)}, u32[]{:S(2)}) collective-permute-start(f32[32,160]{1,0:T(8,128)S(1)} %get-tuple-element.160), channel_id=1, source_target_pairs={{0,8},{8,16},{16,24},{24,32},{32,40},{40,48},{48,56},{56,64},{64,7... | collective-permute-start | bytes 61448 | tf_op jit(solution)/shard_map/while/body/eval_jaxpr/ppermute | solution.py:10
  212.3 11.7 %collective-permute-start.2 = (f32[32,160]{1,0:T(8,128)S(1)}, f32[32,160]{1,0:T(8,128)S(1)}, u32[]{:S(2)}, u32[]{:S(2)}) collective-permute-start(f32[32,160]{1,0:T(8,128)S(1)} %broadcast_select_fusion.2), channel_id=1, source_target_pairs={{0,8},{8,16},{16,24},{24,32},{32,40},{40,48},{48,56},{56,64},{64,7... | collective-permute-start | bytes 61448 | tf_op jit(solution)/shard_map/while/body/eval_jaxpr/ppermute | solution.py:10
  214.2 9.1 %collective-permute-start.1 = (f32[32,160]{1,0:T(8,128)S(1)}, f32[32,160]{1,0:T(8,128)S(1)}, u32[]{:S(2)}, u32[]{:S(2)}) collective-permute-start(f32[32,160]{1,0:T(8,128)S(1)} %get-tuple-element.160), channel_id=1, source_target_pairs={{0,8},{8,16},{16,24},{24,32},{32,40},{40,48},{48,56},{56,64},{64,7... | collective-permute-start | bytes 61448 | tf_op jit(solution)/shard_map/while/body/eval_jaxpr/ppermute | solution.py:10
  226.7 11.7 %collective-permute-start.2 = (f32[32,160]{1,0:T(8,128)S(1)}, f32[32,160]{1,0:T(8,128)S(1)}, u32[]{:S(2)}, u32[]{:S(2)}) collective-permute-start(f32[32,160]{1,0:T(8,128)S(1)} %broadcast_select_fusion.2), channel_id=1, source_target_pairs={{0,8},{8,16},{16,24},{24,32},{32,40},{40,48},{48,56},{56,64},{64,7... | collective-permute-start | bytes 61448 | tf_op jit(solution)/shard_map/while/body/eval_jaxpr/ppermute | solution.py:10
  228.7 9.1 %collective-permute-start.1 = (f32[32,160]{1,0:T(8,128)S(1)}, f32[32,160]{1,0:T(8,128)S(1)}, u32[]{:S(2)}, u32[]{:S(2)}) collective-permute-start(f32[32,160]{1,0:T(8,128)S(1)} %get-tuple-element.160), channel_id=1, source_target_pairs={{0,8},{8,16},{16,24},{24,32},{32,40},{40,48},{48,56},{56,64},{64,7... | collective-permute-start | bytes 61448 | tf_op jit(solution)/shard_map/while/body/eval_jaxpr/ppermute | solution.py:10
  241.2 11.7 %collective-permute-start.2 = (f32[32,160]{1,0:T(8,128)S(1)}, f32[32,160]{1,0:T(8,128)S(1)}, u32[]{:S(2)}, u32[]{:S(2)}) collective-permute-start(f32[32,160]{1,0:T(8,128)S(1)} %broadcast_select_fusion.2), channel_id=1, source_target_pairs={{0,8},{8,16},{16,24},{24,32},{32,40},{40,48},{48,56},{56,64},{64,7... | collective-permute-start | bytes 61448 | tf_op jit(solution)/shard_map/while/body/eval_jaxpr/ppermute | solution.py:10
  243.2 9.1 %collective-permute-start.1 = (f32[32,160]{1,0:T(8,128)S(1)}, f32[32,160]{1,0:T(8,128)S(1)}, u32[]{:S(2)}, u32[]{:S(2)}) collective-permute-start(f32[32,160]{1,0:T(8,128)S(1)} %get-tuple-element.160), channel_id=1, source_target_pairs={{0,8},{8,16},{16,24},{24,32},{32,40},{40,48},{48,56},{56,64},{64,7... | collective-permute-start | bytes 61448 | tf_op jit(solution)/shard_map/while/body/eval_jaxpr/ppermute | solution.py:10
  255.7 11.7 %collective-permute-start.2 = (f32[32,160]{1,0:T(8,128)S(1)}, f32[32,160]{1,0:T(8,128)S(1)}, u32[]{:S(2)}, u32[]{:S(2)}) collective-permute-start(f32[32,160]{1,0:T(8,128)S(1)} %broadcast_select_fusion.2), channel_id=1, source_target_pairs={{0,8},{8,16},{16,24},{24,32},{32,40},{40,48},{48,56},{56,64},{64,7... | collective-permute-start | bytes 61448 | tf_op jit(solution)/shard_map/while/body/eval_jaxpr/ppermute | solution.py:10
  257.7 9.1 %collective-permute-start.1 = (f32[32,160]{1,0:T(8,128)S(1)}, f32[32,160]{1,0:T(8,128)S(1)}, u32[]{:S(2)}, u32[]{:S(2)}) collective-permute-start(f32[32,160]{1,0:T(8,128)S(1)} %get-tuple-element.160), channel_id=1, source_target_pairs={{0,8},{8,16},{16,24},{24,32},{32,40},{40,48},{48,56},{56,64},{64,7... | collective-permute-start | bytes 61448 | tf_op jit(solution)/shard_map/while/body/eval_jaxpr/ppermute | solution.py:10
  270.2 11.7 %collective-permute-start.2 = (f32[32,160]{1,0:T(8,128)S(1)}, f32[32,160]{1,0:T(8,128)S(1)}, u32[]{:S(2)}, u32[]{:S(2)}) collective-permute-start(f32[32,160]{1,0:T(8,128)S(1)} %broadcast_select_fusion.2), channel_id=1, source_target_pairs={{0,8},{8,16},{16,24},{24,32},{32,40},{40,48},{48,56},{56,64},{64,7... | collective-permute-start | bytes 61448 | tf_op jit(solution)/shard_map/while/body/eval_jaxpr/ppermute | solution.py:10
  272.1 9.1 %collective-permute-start.1 = (f32[32,160]{1,0:T(8,128)S(1)}, f32[32,160]{1,0:T(8,128)S(1)}, u32[]{:S(2)}, u32[]{:S(2)}) collective-permute-start(f32[32,160]{1,0:T(8,128)S(1)} %get-tuple-element.160), channel_id=1, source_target_pairs={{0,8},{8,16},{16,24},{24,32},{32,40},{40,48},{48,56},{56,64},{64,7... | collective-permute-start | bytes 61448 | tf_op jit(solution)/shard_map/while/body/eval_jaxpr/ppermute | solution.py:10
  284.7 11.7 %collective-permute-start.2 = (f32[32,160]{1,0:T(8,128)S(1)}, f32[32,160]{1,0:T(8,128)S(1)}, u32[]{:S(2)}, u32[]{:S(2)}) collective-permute-start(f32[32,160]{1,0:T(8,128)S(1)} %broadcast_select_fusion.2), channel_id=1, source_target_pairs={{0,8},{8,16},{16,24},{24,32},{32,40},{40,48},{48,56},{56,64},{64,7... | collective-permute-start | bytes 61448 | tf_op jit(solution)/shard_map/while/body/eval_jaxpr/ppermute | solution.py:10
  286.6 9.1 %collective-permute-start.1 = (f32[32,160]{1,0:T(8,128)S(1)}, f32[32,160]{1,0:T(8,128)S(1)}, u32[]{:S(2)}, u32[]{:S(2)}) collective-permute-start(f32[32,160]{1,0:T(8,128)S(1)} %get-tuple-element.160), channel_id=1, source_target_pairs={{0,8},{8,16},{16,24},{24,32},{32,40},{40,48},{48,56},{56,64},{64,7... | collective-permute-start | bytes 61448 | tf_op jit(solution)/shard_map/while/body/eval_jaxpr/ppermute | solution.py:10
  299.2 11.7 %collective-permute-start.2 = (f32[32,160]{1,0:T(8,128)S(1)}, f32[32,160]{1,0:T(8,128)S(1)}, u32[]{:S(2)}, u32[]{:S(2)}) collective-permute-start(f32[32,160]{1,0:T(8,128)S(1)} %broadcast_select_fusion.2), channel_id=1, source_target_pairs={{0,8},{8,16},{16,24},{24,32},{32,40},{40,48},{48,56},{56,64},{64,7... | collective-permute-start | bytes 61448 | tf_op jit(solution)/shard_map/while/body/eval_jaxpr/ppermute | solution.py:10
  301.1 9.1 %collective-permute-start.1 = (f32[32,160]{1,0:T(8,128)S(1)}, f32[32,160]{1,0:T(8,128)S(1)}, u32[]{:S(2)}, u32[]{:S(2)}) collective-permute-start(f32[32,160]{1,0:T(8,128)S(1)} %get-tuple-element.160), channel_id=1, source_target_pairs={{0,8},{8,16},{16,24},{24,32},{32,40},{40,48},{48,56},{56,64},{64,7... | collective-permute-start | bytes 61448 | tf_op jit(solution)/shard_map/while/body/eval_jaxpr/ppermute | solution.py:10
  313.7 11.7 %collective-permute-start.2 = (f32[32,160]{1,0:T(8,128)S(1)}, f32[32,160]{1,0:T(8,128)S(1)}, u32[]{:S(2)}, u32[]{:S(2)}) collective-permute-start(f32[32,160]{1,0:T(8,128)S(1)} %broadcast_select_fusion.2), channel_id=1, source_target_pairs={{0,8},{8,16},{16,24},{24,32},{32,40},{40,48},{48,56},{56,64},{64,7... | collective-permute-start | bytes 61448 | tf_op jit(solution)/shard_map/while/body/eval_jaxpr/ppermute | solution.py:10
  315.6 9.1 %collective-permute-start.1 = (f32[32,160]{1,0:T(8,128)S(1)}, f32[32,160]{1,0:T(8,128)S(1)}, u32[]{:S(2)}, u32[]{:S(2)}) collective-permute-start(f32[32,160]{1,0:T(8,128)S(1)} %get-tuple-element.160), channel_id=1, source_target_pairs={{0,8},{8,16},{16,24},{24,32},{32,40},{40,48},{48,56},{56,64},{64,7... | collective-permute-start | bytes 61448 | tf_op jit(solution)/shard_map/while/body/eval_jaxpr/ppermute | solution.py:10
  328.2 11.7 %collective-permute-start.2 = (f32[32,160]{1,0:T(8,128)S(1)}, f32[32,160]{1,0:T(8,128)S(1)}, u32[]{:S(2)}, u32[]{:S(2)}) collective-permute-start(f32[32,160]{1,0:T(8,128)S(1)} %broadcast_select_fusion.2), channel_id=1, source_target_pairs={{0,8},{8,16},{16,24},{24,32},{32,40},{40,48},{48,56},{56,64},{64,7... | collective-permute-start | bytes 61448 | tf_op jit(solution)/shard_map/while/body/eval_jaxpr/ppermute | solution.py:10
  330.1 9.1 %collective-permute-start.1 = (f32[32,160]{1,0:T(8,128)S(1)}, f32[32,160]{1,0:T(8,128)S(1)}, u32[]{:S(2)}, u32[]{:S(2)}) collective-permute-start(f32[32,160]{1,0:T(8,128)S(1)} %get-tuple-element.160), channel_id=1, source_target_pairs={{0,8},{8,16},{16,24},{24,32},{32,40},{40,48},{48,56},{56,64},{64,7... | collective-permute-start | bytes 61448 | tf_op jit(solution)/shard_map/while/body/eval_jaxpr/ppermute | solution.py:10
  342.6 11.7 %collective-permute-start.2 = (f32[32,160]{1,0:T(8,128)S(1)}, f32[32,160]{1,0:T(8,128)S(1)}, u32[]{:S(2)}, u32[]{:S(2)}) collective-permute-start(f32[32,160]{1,0:T(8,128)S(1)} %broadcast_select_fusion.2), channel_id=1, source_target_pairs={{0,8},{8,16},{16,24},{24,32},{32,40},{40,48},{48,56},{56,64},{64,7... | collective-permute-start | bytes 61448 | tf_op jit(solution)/shard_map/while/body/eval_jaxpr/ppermute | solution.py:10
  344.6 9.1 %collective-permute-start.1 = (f32[32,160]{1,0:T(8,128)S(1)}, f32[32,160]{1,0:T(8,128)S(1)}, u32[]{:S(2)}, u32[]{:S(2)}) collective-permute-start(f32[32,160]{1,0:T(8,128)S(1)} %get-tuple-element.160), channel_id=1, source_target_pairs={{0,8},{8,16},{16,24},{24,32},{32,40},{40,48},{48,56},{56,64},{64,7... | collective-permute-start | bytes 61448 | tf_op jit(solution)/shard_map/while/body/eval_jaxpr/ppermute | solution.py:10
  357.1 11.7 %collective-permute-start.2 = (f32[32,160]{1,0:T(8,128)S(1)}, f32[32,160]{1,0:T(8,128)S(1)}, u32[]{:S(2)}, u32[]{:S(2)}) collective-permute-start(f32[32,160]{1,0:T(8,128)S(1)} %broadcast_select_fusion.2), channel_id=1, source_target_pairs={{0,8},{8,16},{16,24},{24,32},{32,40},{40,48},{48,56},{56,64},{64,7... | collective-permute-start | bytes 61448 | tf_op jit(solution)/shard_map/while/body/eval_jaxpr/ppermute | solution.py:10
  359.1 9.1 %collective-permute-start.1 = (f32[32,160]{1,0:T(8,128)S(1)}, f32[32,160]{1,0:T(8,128)S(1)}, u32[]{:S(2)}, u32[]{:S(2)}) collective-permute-start(f32[32,160]{1,0:T(8,128)S(1)} %get-tuple-element.160), channel_id=1, source_target_pairs={{0,8},{8,16},{16,24},{24,32},{32,40},{40,48},{48,56},{56,64},{64,7... | collective-permute-start | bytes 61448 | tf_op jit(solution)/shard_map/while/body/eval_jaxpr/ppermute | solution.py:10
  371.6 11.7 %collective-permute-start.2 = (f32[32,160]{1,0:T(8,128)S(1)}, f32[32,160]{1,0:T(8,128)S(1)}, u32[]{:S(2)}, u32[]{:S(2)}) collective-permute-start(f32[32,160]{1,0:T(8,128)S(1)} %broadcast_select_fusion.2), channel_id=1, source_target_pairs={{0,8},{8,16},{16,24},{24,32},{32,40},{40,48},{48,56},{56,64},{64,7... | collective-permute-start | bytes 61448 | tf_op jit(solution)/shard_map/while/body/eval_jaxpr/ppermute | solution.py:10
  373.6 9.1 %collective-permute-start.1 = (f32[32,160]{1,0:T(8,128)S(1)}, f32[32,160]{1,0:T(8,128)S(1)}, u32[]{:S(2)}, u32[]{:S(2)}) collective-permute-start(f32[32,160]{1,0:T(8,128)S(1)} %get-tuple-element.160), channel_id=1, source_target_pairs={{0,8},{8,16},{16,24},{24,32},{32,40},{40,48},{48,56},{56,64},{64,7... | collective-permute-start | bytes 61448 | tf_op jit(solution)/shard_map/while/body/eval_jaxpr/ppermute | solution.py:10
  386.1 11.7 %collective-permute-start.2 = (f32[32,160]{1,0:T(8,128)S(1)}, f32[32,160]{1,0:T(8,128)S(1)}, u32[]{:S(2)}, u32[]{:S(2)}) collective-permute-start(f32[32,160]{1,0:T(8,128)S(1)} %broadcast_select_fusion.2), channel_id=1, source_target_pairs={{0,8},{8,16},{16,24},{24,32},{32,40},{40,48},{48,56},{56,64},{64,7... | collective-permute-start | bytes 61448 | tf_op jit(solution)/shard_map/while/body/eval_jaxpr/ppermute | solution.py:10
  388.0 9.1 %collective-permute-start.1 = (f32[32,160]{1,0:T(8,128)S(1)}, f32[32,160]{1,0:T(8,128)S(1)}, u32[]{:S(2)}, u32[]{:S(2)}) collective-permute-start(f32[32,160]{1,0:T(8,128)S(1)} %get-tuple-element.160), channel_id=1, source_target_pairs={{0,8},{8,16},{16,24},{24,32},{32,40},{40,48},{48,56},{56,64},{64,7... | collective-permute-start | bytes 61448 | tf_op jit(solution)/shard_map/while/body/eval_jaxpr/ppermute | solution.py:10
  400.6 11.7 %collective-permute-start.2 = (f32[32,160]{1,0:T(8,128)S(1)}, f32[32,160]{1,0:T(8,128)S(1)}, u32[]{:S(2)}, u32[]{:S(2)}) collective-permute-start(f32[32,160]{1,0:T(8,128)S(1)} %broadcast_select_fusion.2), channel_id=1, source_target_pairs={{0,8},{8,16},{16,24},{24,32},{32,40},{40,48},{48,56},{56,64},{64,7... | collective-permute-start | bytes 61448 | tf_op jit(solution)/shard_map/while/body/eval_jaxpr/ppermute | solution.py:10
  402.5 9.1 %collective-permute-start.1 = (f32[32,160]{1,0:T(8,128)S(1)}, f32[32,160]{1,0:T(8,128)S(1)}, u32[]{:S(2)}, u32[]{:S(2)}) collective-permute-start(f32[32,160]{1,0:T(8,128)S(1)} %get-tuple-element.160), channel_id=1, source_target_pairs={{0,8},{8,16},{16,24},{24,32},{32,40},{40,48},{48,56},{56,64},{64,7... | collective-permute-start | bytes 61448 | tf_op jit(solution)/shard_map/while/body/eval_jaxpr/ppermute | solution.py:10
  415.1 11.7 %collective-permute-start.2 = (f32[32,160]{1,0:T(8,128)S(1)}, f32[32,160]{1,0:T(8,128)S(1)}, u32[]{:S(2)}, u32[]{:S(2)}) collective-permute-start(f32[32,160]{1,0:T(8,128)S(1)} %broadcast_select_fusion.2), channel_id=1, source_target_pairs={{0,8},{8,16},{16,24},{24,32},{32,40},{40,48},{48,56},{56,64},{64,7... | collective-permute-start | bytes 61448 | tf_op jit(solution)/shard_map/while/body/eval_jaxpr/ppermute | solution.py:10
  417.0 9.1 %collective-permute-start.1 = (f32[32,160]{1,0:T(8,128)S(1)}, f32[32,160]{1,0:T(8,128)S(1)}, u32[]{:S(2)}, u32[]{:S(2)}) collective-permute-start(f32[32,160]{1,0:T(8,128)S(1)} %get-tuple-element.160), channel_id=1, source_target_pairs={{0,8},{8,16},{16,24},{24,32},{32,40},{40,48},{48,56},{56,64},{64,7... | collective-permute-start | bytes 61448 | tf_op jit(solution)/shard_map/while/body/eval_jaxpr/ppermute | solution.py:10
  429.6 11.7 %collective-permute-start.2 = (f32[32,160]{1,0:T(8,128)S(1)}, f32[32,160]{1,0:T(8,128)S(1)}, u32[]{:S(2)}, u32[]{:S(2)}) collective-permute-start(f32[32,160]{1,0:T(8,128)S(1)} %broadcast_select_fusion.2), channel_id=1, source_target_pairs={{0,8},{8,16},{16,24},{24,32},{32,40},{40,48},{48,56},{56,64},{64,7... | collective-permute-start | bytes 61448 | tf_op jit(solution)/shard_map/while/body/eval_jaxpr/ppermute | solution.py:10
  444.1 11.7 %collective-permute-start.2 = (f32[32,160]{1,0:T(8,128)S(1)}, f32[32,160]{1,0:T(8,128)S(1)}, u32[]{:S(2)}, u32[]{:S(2)}) collective-permute-start(f32[32,160]{1,0:T(8,128)S(1)} %broadcast_select_fusion.2), channel_id=1, source_target_pairs={{0,8},{8,16},{16,24},{24,32},{32,40},{40,48},{48,56},{56,64},{64,7... | collective-permute-start | bytes 61448 | tf_op jit(solution)/shard_map/while/body/eval_jaxpr/ppermute | solution.py:10
  458.6 11.7 %collective-permute-start.2 = (f32[32,160]{1,0:T(8,128)S(1)}, f32[32,160]{1,0:T(8,128)S(1)}, u32[]{:S(2)}, u32[]{:S(2)}) collective-permute-start(f32[32,160]{1,0:T(8,128)S(1)} %broadcast_select_fusion.2), channel_id=1, source_target_pairs={{0,8},{8,16},{16,24},{24,32},{32,40},{40,48},{48,56},{56,64},{64,7... | collective-permute-start | bytes 61448 | tf_op jit(solution)/shard_map/while/body/eval_jaxpr/ppermute | solution.py:10
  460.5 9.1 %collective-permute-start.1 = (f32[32,160]{1,0:T(8,128)S(1)}, f32[32,160]{1,0:T(8,128)S(1)}, u32[]{:S(2)}, u32[]{:S(2)}) collective-permute-start(f32[32,160]{1,0:T(8,128)S(1)} %get-tuple-element.160), channel_id=1, source_target_pairs={{0,8},{8,16},{16,24},{24,32},{32,40},{40,48},{48,56},{56,64},{64,7... | collective-permute-start | bytes 61448 | tf_op jit(solution)/shard_map/while/body/eval_jaxpr/ppermute | solution.py:10
  473.0 11.7 %collective-permute-start.2 = (f32[32,160]{1,0:T(8,128)S(1)}, f32[32,160]{1,0:T(8,128)S(1)}, u32[]{:S(2)}, u32[]{:S(2)}) collective-permute-start(f32[32,160]{1,0:T(8,128)S(1)} %broadcast_select_fusion.2), channel_id=1, source_target_pairs={{0,8},{8,16},{16,24},{24,32},{32,40},{40,48},{48,56},{56,64},{64,7... | collective-permute-start | bytes 61448 | tf_op jit(solution)/shard_map/while/body/eval_jaxpr/ppermute | solution.py:10
  475.0 9.1 %collective-permute-start.1 = (f32[32,160]{1,0:T(8,128)S(1)}, f32[32,160]{1,0:T(8,128)S(1)}, u32[]{:S(2)}, u32[]{:S(2)}) collective-permute-start(f32[32,160]{1,0:T(8,128)S(1)} %get-tuple-element.160), channel_id=1, source_target_pairs={{0,8},{8,16},{16,24},{24,32},{32,40},{40,48},{48,56},{56,64},{64,7... | collective-permute-start | bytes 61448 | tf_op jit(solution)/shard_map/while/body/eval_jaxpr/ppermute | solution.py:10
  487.5 11.7 %collective-permute-start.2 = (f32[32,160]{1,0:T(8,128)S(1)}, f32[32,160]{1,0:T(8,128)S(1)}, u32[]{:S(2)}, u32[]{:S(2)}) collective-permute-start(f32[32,160]{1,0:T(8,128)S(1)} %broadcast_select_fusion.2), channel_id=1, source_target_pairs={{0,8},{8,16},{16,24},{24,32},{32,40},{40,48},{48,56},{56,64},{64,7... | collective-permute-start | bytes 61448 | tf_op jit(solution)/shard_map/while/body/eval_jaxpr/ppermute | solution.py:10
  489.5 9.1 %collective-permute-start.1 = (f32[32,160]{1,0:T(8,128)S(1)}, f32[32,160]{1,0:T(8,128)S(1)}, u32[]{:S(2)}, u32[]{:S(2)}) collective-permute-start(f32[32,160]{1,0:T(8,128)S(1)} %get-tuple-element.160), channel_id=1, source_target_pairs={{0,8},{8,16},{16,24},{24,32},{32,40},{40,48},{48,56},{56,64},{64,7... | collective-permute-start | bytes 61448 | tf_op jit(solution)/shard_map/while/body/eval_jaxpr/ppermute | solution.py:10
  502.0 11.7 %collective-permute-start.2 = (f32[32,160]{1,0:T(8,128)S(1)}, f32[32,160]{1,0:T(8,128)S(1)}, u32[]{:S(2)}, u32[]{:S(2)}) collective-permute-start(f32[32,160]{1,0:T(8,128)S(1)} %broadcast_select_fusion.2), channel_id=1, source_target_pairs={{0,8},{8,16},{16,24},{24,32},{32,40},{40,48},{48,56},{56,64},{64,7... | collective-permute-start | bytes 61448 | tf_op jit(solution)/shard_map/while/body/eval_jaxpr/ppermute | solution.py:10
  503.9 9.1 %collective-permute-start.1 = (f32[32,160]{1,0:T(8,128)S(1)}, f32[32,160]{1,0:T(8,128)S(1)}, u32[]{:S(2)}, u32[]{:S(2)}) collective-permute-start(f32[32,160]{1,0:T(8,128)S(1)} %get-tuple-element.160), channel_id=1, source_target_pairs={{0,8},{8,16},{16,24},{24,32},{32,40},{40,48},{48,56},{56,64},{64,7... | collective-permute-start | bytes 61448 | tf_op jit(solution)/shard_map/while/body/eval_jaxpr/ppermute | solution.py:10
  516.5 9.4 %collective-permute-start.3 = (f32[32,160]{1,0:T(8,128)S(1)}, f32[32,160]{1,0:T(8,128)S(1)}, u32[]{:S(2)}, u32[]{:S(2)}) collective-permute-start(f32[32,160]{1,0:T(8,128)S(1)} %get-tuple-element.51), channel_id=1, source_target_pairs={{0,8},{8,16},{16,24},{24,32},{32,40},{40,48},{48,56},{56,64},{64,7... | collective-permute-start | bytes 61448 | tf_op jit(solution)/shard_map/ppermute | solution.py:10
  528.2 94.6 %collective-permute-start.5 = (f32[32,160]{1,0:T(8,128)S(1)}, f32[32,160]{1,0:T(8,128)S(1)}, u32[]{:S(2)}, u32[]{:S(2)}) collective-permute-start(f32[32,160]{1,0:T(8,128)S(1)} %get-tuple-element.53), channel_id=1, source_target_pairs={{0,264},{8,272},{16,280},{24,288},{32,296},{40,304},{48,312},{56,3... | collective-permute-start | bytes 61448 | tf_op jit(solution)/shard_map/ppermute | solution.py:10
  (36 other events, 306.8 us)
Sparse Core Ops, SparseCore 0:
  528.3 93.5 reduce-scatter.3
